TPU v7x, 512 devices: a whole 4x8x8 slice. The times are simulated.
512 devices in a mesh: section: 8 (over z_hi, x), ctx: 64 (over y, z_lo, core).
Axes of the slice: x: 4, y: 8, z: 8 (z_hi: 2, z_lo: 4; z = z_hi * 4 + z_lo), core: 2. Of those that a mesh axis runs over, the one named last changes fastest.
Arguments:
- resid: bfloat16 [8, 16384, 4096], P('section', 'ctx'), may hold values from -16 to 16
- queries: bfloat16 [8, 16384, 512], P('section', 'ctx'), may hold values from -8 to 8
- keyvals: bfloat16 [8, 16384, 256], P('section', 'ctx'), may hold values from -8 to 8
- run_max: float32 [8, 16384, 4], P('section', 'ctx'), may hold values from 1 to 4
- run_sum: float32 [8, 16384, 4], P('section', 'ctx'), may hold values from 128 to 1024
- run_out: float32 [8, 16384, 512], P('section', 'ctx'), may hold values from -384 to 384
- span_pair: int32 [64, 2], replicated, may hold values from 0 to 127, as said below
- norm_gain: float32 [8, 4096], P('section'), may hold values from 0.5 to 1.5
- w_query: bfloat16 [8, 4096, 512], P('section', 'ctx'), may hold values from -0.095458984 to 0.095458984
- w_keyval: bfloat16 [8, 4096, 256], P('section', 'ctx'), may hold values from -0.095458984 to 0.095458984
- w_out: bfloat16 [8, 512, 4096], P('section', None, 'ctx'), may hold values from -0.59765625 to 0.59765625
Outputs:
- queries_next: bfloat16 [8, 16384, 512], P('section', 'ctx')
- keyvals_next: bfloat16 [8, 16384, 256], P('section', 'ctx')
- max_next: float32 [8, 16384, 4], P('section', 'ctx')
- sum_next: float32 [8, 16384, 4], P('section', 'ctx')
- out_next: float32 [8, 16384, 512], P('section', 'ctx')
Inputs may be any that keep to these rules, and one draw needn't show every extreme that they name: `span_pair`: each ctx index holds blocks c and 127 - c, its first column running once over 0 to 63.
All inputs are finite; a program needn't handle non-finite values.
Results may differ from a plain program's by a relative error of at most 0.005.
The roundings to bfloat16 on the way count: a program that leaves them out, or rounds other values in their place, can miss the bound.
Values may be sent and summed in bfloat16 or wider, within the bound.
No kernel may reach another device: no remote copies, remote signals or barrier semaphores. Data moves between devices by JAX's collectives and lax.ppermute only.
A program may use at most 64 MiB of HBM per device.

v0:
```python
import jax
import jax.numpy as jnp
from jax import lax
from jax.sharding import PartitionSpec as P

HEAD = 128
QHEADS = 4


def passed_along(value, axis, steps):
    count = lax.axis_size(axis)
    pairs = [(source, (source + steps) % count) for source in range(count)]
    return lax.ppermute(value, axis, pairs)


def device_positions(span_pair, device, rows_here):
    half_rows = rows_here // 2
    span_row = lax.dynamic_slice_in_dim(span_pair, device, 1, 0)[0]
    offsets = jnp.arange(rows_here, dtype=jnp.int32)
    span_index = jnp.where(offsets < half_rows, span_row[0], span_row[1])
    return span_index * half_rows + offsets % half_rows


def flash_step(query_rows, key_block, pos_query, pos_key, old_max, old_sum, old_out):
    rows_here = query_rows.shape[0]
    query_heads = query_rows.reshape(rows_here, QHEADS, HEAD)
    key_part = key_block[:, :HEAD]
    value_part = key_block[:, HEAD:]
    scores = jnp.einsum(
        "qhd,kd->hqk", query_heads, key_part, preferred_element_type=jnp.float32
    ) * HEAD ** (-0.5)
    keep = pos_key[None, None, :] <= pos_query[None, :, None]
    masked = jnp.where(keep, scores, -1e30)
    prior_max = old_max.T
    new_max = jnp.maximum(prior_max, jnp.max(masked, axis=-1))
    exp_scores = jnp.where(keep, jnp.exp(scores - new_max[:, :, None]), 0.0)
    decay_factor = jnp.exp(prior_max - new_max)
    new_sum = old_sum.T * decay_factor + jnp.sum(exp_scores, axis=-1)
    rounded = exp_scores.astype(jnp.bfloat16)
    contrib = jnp.einsum("hqk,kd->qhd", rounded, value_part, preferred_element_type=jnp.float32)
    new_out = old_out.reshape(rows_here, QHEADS, HEAD) * decay_factor.T[:, :, None] + contrib
    return (new_max.T, new_sum.T, new_out.reshape(rows_here, QHEADS * HEAD))


def add_rows(normed, shard_rows):
    return jnp.dot(normed, shard_rows, preferred_element_type=jnp.float32)


def per_device(
    resid,
    queries,
    keyvals,
    run_max,
    run_sum,
    run_out,
    span_pair,
    norm_gain,
    w_query,
    w_keyval,
    w_out,
):
    cycle_size = lax.axis_size("ctx")
    my_index = lax.axis_index("ctx")
    rows_here = resid.shape[1]
    pos_mine = device_positions(span_pair, my_index, rows_here)
    pos_near = device_positions(span_pair, (my_index + 1) % cycle_size, rows_here)
    pos_far = device_positions(span_pair, (my_index + 2) % cycle_size, rows_here)
    keyval_own = keyvals[0]
    near_block = passed_along(keyval_own, "ctx", -1)
    far_block = passed_along(near_block, "ctx", -1)
    max_now, sum_now, out_now = flash_step(
        queries[0], far_block, pos_mine, pos_far, run_max[0], run_sum[0], run_out[0]
    )
    max_now, sum_now, out_now = flash_step(
        queries[0], near_block, pos_mine, pos_near, max_now, sum_now, out_now
    )
    divided = out_now.reshape(rows_here, QHEADS, HEAD) / sum_now[:, :, None]
    attended = divided.reshape(rows_here, QHEADS * HEAD).astype(jnp.bfloat16)
    projected = jnp.dot(
        attended,
        lax.all_gather(w_out[0], "ctx", axis=1, tiled=True),
        preferred_element_type=jnp.float32,
    )
    finished = (resid[0].astype(jnp.float32) + projected).astype(jnp.bfloat16)
    incoming = passed_along(finished, "section", 1)
    wide = incoming.astype(jnp.float32)
    mean_square = jnp.mean(wide * wide, axis=-1, keepdims=True)
    normed = (wide * lax.rsqrt(mean_square + 1e-05) * norm_gain[0][None, :]).astype(jnp.bfloat16)

    def add_one(shard_rows):
        return add_rows(normed, shard_rows)

    query_sum = add_one(lax.all_gather(w_query[0], "ctx", axis=0, tiled=True))
    keyval_sum = add_one(lax.all_gather(w_keyval[0], "ctx", axis=0, tiled=True))
    query_new = query_sum.astype(jnp.bfloat16)
    keyval_new = keyval_sum.astype(jnp.bfloat16)
    start_max = jnp.full((rows_here, QHEADS), -1e30, jnp.float32)
    start_sum = jnp.zeros((rows_here, QHEADS), jnp.float32)
    start_out = jnp.zeros((rows_here, QHEADS * HEAD), jnp.float32)
    max_new, sum_new, out_new = flash_step(
        query_new, keyval_new, pos_mine, pos_mine, start_max, start_sum, start_out
    )
    return (query_new[None], keyval_new[None], max_new[None], sum_new[None], out_new[None])


def solution(mesh):
    placed = (
        P("section", "ctx", None),
        P("section", "ctx", None),
        P("section", "ctx", None),
        P("section", "ctx", None),
        P("section", "ctx", None),
        P("section", "ctx", None),
        P(),
        P("section", None),
        P("section", "ctx", None),
        P("section", "ctx", None),
        P("section", None, "ctx"),
    )
    return jax.shard_map(
        per_device,
        mesh=mesh,
        in_specs=placed,
        out_specs=(
            P("section", "ctx", None),
            P("section", "ctx", None),
            P("section", "ctx", None),
            P("section", "ctx", None),
            P("section", "ctx", None),
        ),
        check_vma=False,
    )
```

profile of v0, /device:TPU:1, one launch (start us, length us, event | category | flops | bytes accessed | tf_op | source)
XLA Modules:
  0.0 459.4 jit_solution(41437203591196475)
XLA Ops:
  7.2 0.0 copy-start.3
  7.2 0.0 copy-start.4
  7.2 0.0 all-gather.7.cloned.1.call-start
  7.2 0.7 all-gather.7.cloned.1.call-update
  7.9 0.0 all-gather.11.cloned.1.call-start
  8.0 0.7 all-gather.11.cloned.1.call-update
  8.7 0.0 all-gather.9.cloned.1.call-start
  8.7 0.7 all-gather.9.cloned.1.call-update
  9.4 8.7 %collective-permute-start = (bf16[256,256]{1,0:T(8,128)(2,1)}, bf16[256,256]{1,0:T(8,128)(2,1)S(1)}, u32[]{:S(2)}, u32[]{:S(2)}) collective-permute-start(bf16[256,256]{1,0:T(8,128)(2,1)} %bitcast.147), channel_id=1, source_target_pairs={{0,63},{1,0},{2,1},{3,2},{4,3},{5,4},{6,5},{7,6},{8,7},{9,8},{10,9... | collective-permute-start | bytes 393224 | tf_op jit(solution)/shard_map/ppermute | solution.py:13
  18.2 1.0 reshape_squeeze.8
  19.2 1.2 copy.16
  20.5 0.9 constant_dynamic-slice_fusion.2
  21.3 0.5 fusion.61
  21.9 1.3 multiply_add_fusion.2
  23.2 0.5 fusion.62
  23.7 0.5 fusion.63
  24.2 2.6 multiply_add_fusion
  26.8 0.2 broadcast_compare_fusion
  27.0 0.0 collective-permute-done
  27.0 4.9 %collective-permute-start.1 = (bf16[256,256]{1,0:T(8,128)(2,1)S(1)}, bf16[256,256]{1,0:T(8,128)(2,1)S(1)}, u32[]{:S(2)}, u32[]{:S(2)}) collective-permute-start(bf16[256,256]{1,0:T(8,128)(2,1)S(1)} %collective-permute-done), channel_id=1, source_target_pairs={{0,63},{1,0},{2,1},{3,2},{4,3},{5,4},{6,5},{7,6},{8,7},{9,8},{10,9... | collective-permute-start | bytes 393224 | tf_op jit(solution)/shard_map/ppermute | solution.py:13
  31.9 0.3 select_reduce_fusion.1
  32.2 1.8 collective-permute-done.1
  34.0 0.3 select_reduce_fusion.2
  34.3 0.0 copy-start
  34.3 0.0 copy-done.3
  34.3 0.2 fusion.24
  34.5 0.2 fusion.26
  34.8 0.0 copy-done.4
  34.8 0.3 convolution_bitcast_fusion.1
  35.1 0.4 fusion.17
  35.5 100.8 %all-gather.7.cloned.1.call-done = bf16[1,512,4096]{1,2,0:T(8,128)(2,1)} async-done(((bf16[1,512,64]{1,2,0:T(8,128)(2,1)}), bf16[1,512,4096]{1,2,0:T(8,128)(2,1)}) %all-gather.7.cloned.1.call-update) | async-done | bytes 4194320 | tf_op jit(solution)/shard_map/all_gather | solution.py:81
  136.3 0.0 copy-done
  136.3 3.5 fusion
  139.8 2.9 collective-permute-start.2
  142.7 102.5 %collective-permute-done.2 = bf16[256,4096]{1,0:T(8,128)(2,1)S(1)} collective-permute-done((bf16[256,4096]{1,0:T(8,128)(2,1)S(1)}, bf16[256,4096]{1,0:T(8,128)(2,1)S(1)}, u32[]{:S(2)}, u32[]{:S(2)}) %collective-permute-start.2) | collective-permute-done | bytes 2097184 | tf_op jit(solution)/shard_map/ppermute | solution.py:13
  245.3 0.5 fusion.1
  245.8 8.6 %all-gather.11.cloned.1.call-done = bf16[1,4096,256]{2,1,0:T(8,128)(2,1)} async-done(((bf16[1,64,256]{2,1,0:T(8,128)(2,1)}), bf16[1,4096,256]{2,1,0:T(8,128)(2,1)}) %all-gather.11.cloned.1.call-update) | async-done | bytes 2097168 | tf_op jit(solution)/shard_map/all_gather | solution.py:94
  254.4 2.4 fusion.21
  256.8 0.0 copy-start.2
  256.8 189.5 %all-gather.9.cloned.1.call-done = bf16[1,4096,512]{2,1,0:T(8,128)(2,1)} async-done(((bf16[1,64,512]{2,1,0:T(8,128)(2,1)}), bf16[1,4096,512]{2,1,0:T(8,128)(2,1)}) %all-gather.9.cloned.1.call-update) | async-done | bytes 4194320 | tf_op jit(solution)/shard_map/all_gather | solution.py:93
  446.3 3.5 fusion.18
  449.8 0.0 copy-start.1
  449.8 0.3 select_reduce_fusion
  450.1 0.6 broadcast_maximum_fusion
  450.7 0.2 fusion.29
  450.9 0.6 fusion.51
  451.5 0.3 fusion.16
  451.9 1.0 copy.26
  (7 shorter events, 0.0 us)
Async XLA Ops:
  7.2 27.2 %copy-start.3 = (f32[1,256,4]{1,2,0:T(4,128)S(1)}, f32[1,256,4]{1,2,0:T(4,128)}, u32[]{:S(2)}) copy-start(f32[1,256,4]{1,2,0:T(4,128)} %param.14) | copy-start | bytes 12292
  7.2 27.6 %copy-start.4 = (f32[1,256,4]{1,2,0:T(4,128)S(1)}, f32[1,256,4]{1,2,0:T(4,128)}, u32[]{:S(2)}) copy-start(f32[1,256,4]{1,2,0:T(4,128)} %param.15) | copy-start | bytes 12292
  7.2 129.1 %all-gather.7.cloned.1.call-start = ((), (), s32[]{:S(2)}) async-start(), calls=%async_computation | async-start | bytes 4259840 | tf_op jit(solution)/shard_map/all_gather | solution.py:81
  7.9 246.4 %all-gather.11.cloned.1.call-start = ((), (), s32[]{:S(2)}) async-start(), calls=%async_computation.2 | async-start | bytes 2129920 | tf_op jit(solution)/shard_map/all_gather | solution.py:94
  8.7 437.6 %all-gather.9.cloned.1.call-start = ((), (), s32[]{:S(2)}) async-start(), calls=%async_computation.1 | async-start | bytes 4259840 | tf_op jit(solution)/shard_map/all_gather | solution.py:93
  9.4 17.6 %collective-permute-start = (bf16[256,256]{1,0:T(8,128)(2,1)}, bf16[256,256]{1,0:T(8,128)(2,1)S(1)}, u32[]{:S(2)}, u32[]{:S(2)}) collective-permute-start(bf16[256,256]{1,0:T(8,128)(2,1)} %bitcast.147), channel_id=1, source_target_pairs={{0,63},{1,0},{2,1},{3,2},{4,3},{5,4},{6,5},{7,6},{8,7},{9,8},{10,9... | collective-permute-start | bytes 393224 | tf_op jit(solution)/shard_map/ppermute | solution.py:13
  27.0 7.0 %collective-permute-start.1 = (bf16[256,256]{1,0:T(8,128)(2,1)S(1)}, bf16[256,256]{1,0:T(8,128)(2,1)S(1)}, u32[]{:S(2)}, u32[]{:S(2)}) collective-permute-start(bf16[256,256]{1,0:T(8,128)(2,1)S(1)} %collective-permute-done), channel_id=1, source_target_pairs={{0,63},{1,0},{2,1},{3,2},{4,3},{5,4},{6,5},{7,6},{8,7},{9,8},{10,9... | collective-permute-start | bytes 393224 | tf_op jit(solution)/shard_map/ppermute | solution.py:13
  34.3 102.0 %copy-start = (bf16[1,256,4096]{2,1,0:T(8,128)(2,1)S(1)}, bf16[1,256,4096]{2,1,0:T(8,128)(2,1)}, u32[]{:S(2)}) copy-start(bf16[1,256,4096]{2,1,0:T(8,128)(2,1)} %param.11) | copy-start | bytes 6291460
  136.3 118.1 %copy-start.5 = (f32[1,4096]{1,0:T(1,128)S(1)}, f32[1,4096]{1,0:T(1,128)}, u32[]{:S(2)}) copy-start(f32[1,4096]{1,0:T(1,128)} %param.18) | copy-start | bytes 49156
  139.8 105.5 %collective-permute-start.2 = (bf16[256,4096]{1,0:T(8,128)(2,1)S(1)}, bf16[256,4096]{1,0:T(8,128)(2,1)S(1)}, u32[]{:S(2)}, u32[]{:S(2)}) collective-permute-start(bf16[256,4096]{1,0:T(8,128)(2,1)S(1)} %fusion), channel_id=1, source_target_pairs={{0,64},{64,128},{128,192},{192,256},{256,320},{320,384},{384,448},... | collective-permute-start | bytes 6291464 | tf_op jit(solution)/shard_map/ppermute | solution.py:13
  256.8 194.8 %copy-start.2 = (bf16[256,256]{1,0:T(8,128)(2,1)}, bf16[256,256]{1,0:T(8,128)(2,1)S(1)}, u32[]{:S(2)}) copy-start(bf16[256,256]{1,0:T(8,128)(2,1)S(1)} %fusion.21) | copy-start | bytes 393220
  449.8 3.1 copy-start.1
Sparse Core Ops, SparseCore 0:
  10.1 126.0 all-gather.6
  138.4 115.9 all-gather.10
  256.5 189.7 all-gather.8
where the time goes:
time: 460 us; the launch traced here: 459 us
  waiting for transfers between devices  405 us (88%)
  starting transfers between devices  16.7 us (4%)
  between operations  14 us (3%)
  matrix products  11.4 us (2%)
  other arithmetic  6.42 us (1%)
  local copies, waits for them, and re-layouts  5.7 us (1%)
    all_gather x1, waiting for transfers between devices, per_device(): query_sum = add_one(lax.all_gather(w_query[0], 'ctx', axis=0, tiled=True))  190 us
    ppermute x3, waiting for transfers between devices, passed_along(): return lax.ppermute(value, axis, pairs)  104 us
    all_gather x1, waiting for transfers between devices, per_device(): lax.all_gather(w_out[0], 'ctx', axis=1, tiled=True)  101 us
    ppermute x3, starting transfers between devices, passed_along(): return lax.ppermute(value, axis, pairs)  16.6 us
  transfers between devices with their start and end apart: 6, of which 5 were waited for; matrix products, arithmetic and copies ran while one was open for 4% of the time, Pallas kernels for 0%

commit v1 on v0

v1 whole, which is shorter than its diff:
```python
import jax
import jax.numpy as jnp
from jax import lax
from jax.experimental import pallas as pl
from jax.experimental.pallas import tpu as pltpu
from jax.sharding import Mesh
from jax.sharding import PartitionSpec as P


HEAD = 128
QHEADS = 4
SECT = ("zh", "x")
CTX = ("y", "zl", "c")
NY, NZ, NC, NS = 8, 4, 2, 8
SHARD = 64
PAIR = 2
NX = 4
CUT = 160
BLOCK = NZ * NC * SHARD
NQ = QHEADS * HEAD
NKV = 2 * HEAD


def ring(count, steps):
    return [(source, (source + steps) % count) for source in range(count)]


def positions(span_ref, device, rows, axis):
    half = rows // 2
    shape = (rows, 1) if axis == 0 else (1, rows)
    offset = lax.broadcasted_iota(jnp.int32, shape, axis)
    first = span_ref[0, device] * half
    second = span_ref[1, device] * half - half
    return offset + jnp.where(offset < half, first, second)


def block_update(query, key, value, keep, old):
    scores = lax.dot_general(
        key, query, (((1,), (1,)), ((), ())), preferred_element_type=jnp.float32
    ) * HEAD ** (-0.5)
    masked = jnp.where(keep, scores, -1e30)
    old_max, old_sum, old_out = old
    new_max = jnp.maximum(old_max, jnp.max(masked, axis=0, keepdims=True))
    exp_scores = jnp.where(keep, jnp.exp(scores - new_max), 0.0)
    decay = jnp.exp(old_max - new_max)
    new_sum = old_sum * decay + jnp.sum(exp_scores, axis=0, keepdims=True)
    contrib = jnp.dot(value, exp_scores.astype(jnp.bfloat16), preferred_element_type=jnp.float32)
    new_out = contrib if old_out is None else old_out * decay + contrib
    return new_max, new_sum, new_out


def attend_kernel(index_ref, span_ref, query_ref, far_ref, near_ref, max_ref, sum_ref, out_ref, att_ref):
    count = NY * NZ * NC
    rows = query_ref.shape[0]
    mine = index_ref[0]
    pos_query = positions(span_ref, mine, rows, 1)
    blocks = []
    for hop, block_ref in ((2, far_ref), (1, near_ref)):
        keep = positions(span_ref, lax.rem(mine + hop, count), rows, 0) <= pos_query
        blocks.append((block_ref[:, :HEAD], block_ref[:, HEAD:].T, keep))
    for h in range(QHEADS):
        cols = slice(h * HEAD, (h + 1) * HEAD)
        state = max_ref[h : h + 1, :], sum_ref[h : h + 1, :], out_ref[:, cols].T
        for block in blocks:
            state = block_update(query_ref[:, cols], *block, state)
        att_ref[:, cols] = (state[2] / state[1]).T.astype(jnp.bfloat16)


def attend(my_index, spans, *operands):
    return pl.pallas_call(
        attend_kernel,
        out_shape=jax.ShapeDtypeStruct(operands[0].shape, jnp.bfloat16),
        in_specs=[pl.BlockSpec(memory_space=pltpu.SMEM)] * 2
        + [pl.BlockSpec(memory_space=pltpu.VMEM)] * len(operands),
        out_specs=pl.BlockSpec(memory_space=pltpu.VMEM),
        name="attend",
    )(my_index, spans, *operands)


def in_order(w_ref, base, slots):
    parts = []
    for z in range(NZ):
        for c in range(NC):
            start = base + (c * NZ + slots[z]) * SHARD
            if not isinstance(start, int):
                start = pl.multiple_of(start, SHARD)
            parts.append(w_ref[pl.ds(start, SHARD), :])
    return parts


def layer_kernel(
    place_ref,
    span_ref,
    att_ref,
    direct_ref,
    near_ref,
    far_ref,
    gain_ref,
    out_a_ref,
    out_b_ref,
    next_ref,
    query_ref,
    keyval_ref,
    max_ref,
    sum_ref,
    wide_ref,
    rows_ref,
    sq_ref,
    acc_ref,
):
    step = pl.program_id(0)
    half = NY // PAIR
    width = PAIR * BLOCK

    @pl.when(step < half)
    def _():
        slots = [lax.rem(place_ref[1] - z + NZ, NZ) for z in range(NZ)]

        def part(w_ref, cols):
            pieces = []
            for k in range(PAIR):
                pieces += in_order(w_ref, k * BLOCK, slots)
            return lax.dot_general(
                att_ref[:, cols],
                jnp.concatenate(pieces, axis=0),
                (((1,), (1,)), ((), ())),
                preferred_element_type=jnp.float32,
            )

        projected = part(out_a_ref, slice(0, NQ // 2)) + part(out_b_ref, slice(NQ // 2, NQ))
        by_near = place_ref[2] > 0
        routed = jnp.where(by_near, near_ref[...], far_ref[...])
        resid = jnp.concatenate([direct_ref[...], routed], axis=0)
        finished = (resid.astype(jnp.float32) + projected).astype(jnp.bfloat16)
        square = finished.astype(jnp.float32)
        square = square * square
        total = sum(square[:, j * HEAD : (j + 1) * HEAD] for j in range(width // HEAD))
        rows_ref[step] = finished

        @pl.when(step == 0)
        def _():
            sq_ref[...] = total

        @pl.when(step > 0)
        def _():
            sq_ref[...] += total

    @pl.when(step == half - 1)
    def _():
        mean = jnp.sum(sq_ref[...], axis=-1, keepdims=True) / (NY * BLOCK)
        scale = lax.rsqrt(mean + 1e-05)
        for k in range(half):
            gain = gain_ref[:, k * width : (k + 1) * width]
            value = rows_ref[k].astype(jnp.float32) * scale * gain
            rows_ref[k] = value.astype(jnp.bfloat16)

    @pl.when(step >= half)
    def _():
        pieces = []
        for k in range(PAIR):
            pieces += in_order(next_ref, k * BLOCK, range(NZ))
        total = jnp.dot(
            rows_ref[step - half],
            jnp.concatenate(pieces, axis=0),
            preferred_element_type=jnp.float32,
        )

        @pl.when(step == half)
        def _():
            acc_ref[...] = total

        @pl.when(step > half)
        def _():
            acc_ref[...] += total

    @pl.when(step == 2 * half - 1)
    def _():
        rows = query_ref.shape[0]
        query_ref[...] = acc_ref[:, :NQ].astype(jnp.bfloat16)
        keyval_ref[...] = acc_ref[:, NQ:].astype(jnp.bfloat16)
        mine = place_ref[0]
        keep = positions(span_ref, mine, rows, 0) <= positions(span_ref, mine, rows, 1)
        key = keyval_ref[:, :HEAD]
        value = keyval_ref[:, HEAD:].T
        for h in range(QHEADS):
            cols = slice(h * HEAD, (h + 1) * HEAD)
            state = jnp.full((1, rows), -1e30, jnp.float32), jnp.zeros((1, rows), jnp.float32), None
            state = block_update(query_ref[:, cols], key, value, keep, state)
            max_ref[h : h + 1, :] = state[0]
            sum_ref[h : h + 1, :] = state[1]
            wide_ref[:, cols] = state[2].T


def layer(place, spans, attended, direct, near, far, gain, weights):
    rows = attended.shape[0]
    half = NY // PAIR
    width = PAIR * BLOCK
    first = lambda i: jnp.minimum(i, half - 1)
    second = lambda i: jnp.maximum(i - half, 0)
    whole = lambda shape: pl.BlockSpec(shape, lambda i, *_: (0,) * len(shape))
    by_cols = lambda v: pl.BlockSpec((v.shape[0], width), lambda i, *_: (0, first(i)))
    out_cols = (NQ + NKV) // (NQ // 2)
    stat = jax.ShapeDtypeStruct((QHEADS, rows), jnp.float32)
    out_shape = (
        jax.ShapeDtypeStruct((rows, NQ), jnp.bfloat16),
        jax.ShapeDtypeStruct((rows, NKV), jnp.bfloat16),
        stat,
        stat,
        jax.ShapeDtypeStruct((rows, NQ), jnp.float32),
    )
    return pl.pallas_call(
        layer_kernel,
        out_shape=out_shape,
        grid_spec=pltpu.PrefetchScalarGridSpec(
            num_scalar_prefetch=2,
            grid=(2 * half,),
            in_specs=[
                whole(attended.shape),
                by_cols(direct),
                by_cols(near),
                by_cols(far),
                whole(gain.shape),
                pl.BlockSpec((width, NQ // 2), lambda i, *_: (first(i), out_cols)),
                pl.BlockSpec((width, NQ // 2), lambda i, *_: (first(i), out_cols + 1)),
                pl.BlockSpec((width, NQ + NKV), lambda i, *_: (second(i), 0)),
            ],
            out_specs=tuple(whole(v.shape) for v in out_shape),
            scratch_shapes=[
                pltpu.VMEM((half, rows, width), jnp.bfloat16),
                pltpu.VMEM((rows, HEAD), jnp.float32),
                pltpu.VMEM((rows, NQ + NKV), jnp.float32),
            ],
        ),
        compiler_params=pltpu.CompilerParams(dimension_semantics=("arbitrary",)),
        name="layer",
    )(place, spans, attended, direct, near, far, gain, weights, weights, weights)


def per_device(
    resid,
    queries,
    keyvals,
    run_max,
    run_sum,
    run_out,
    span_pair,
    norm_gain,
    w_query,
    w_keyval,
    w_out,
):
    count = NY * NZ * NC
    my_index = lax.axis_index(CTX).astype(jnp.int32)
    my_z = lax.axis_index("zl").astype(jnp.int32)
    my_x = lax.axis_index("x").astype(jnp.int32)
    spans = span_pair.T

    out_parts = []
    for k in range(NZ):
        pairs = [
            (s * NZ + z, (s + 1) % NS * NZ + (z + k) % NZ) for s in range(NS) for z in range(NZ)
        ]
        out_parts.append(lax.ppermute(w_out[0].T, (*SECT, "zl"), pairs))
    near_block = lax.ppermute(keyvals[0], CTX, ring(count, -1))
    far_block = lax.ppermute(keyvals[0], CTX, ring(count, -2))

    next_shard = jnp.concatenate([w_query[0], w_keyval[0]], axis=1)
    next_copies = jnp.broadcast_to(next_shard, (NZ, SHARD, NQ + NKV))
    next_rows = lax.all_to_all(next_copies, "zl", 0, 0, tiled=True).reshape(NZ * SHARD, NQ + NKV)
    shards = jnp.concatenate([next_rows, jnp.concatenate(out_parts)], axis=1)
    weights = lax.all_gather(shards, ("y", "c"), axis=0, tiled=True)

    rest = resid[0, CUT:]
    wrap = NX - 1
    turn = [(s, s + 1) for s in range(NS) if s % NX < wrap - 1]
    turn += [(s, (s + NX) % NS) for s in range(NS) if s % NX == wrap]
    near = lax.ppermute(rest, SECT, turn)
    direct = lax.ppermute(resid[0, :CUT], SECT, ring(NS, 1))
    attended = attend(
        my_index.reshape(1), spans, queries[0], far_block, near_block,
        run_max[0].T, run_sum[0].T, run_out[0],
    )
    attended_sent = lax.ppermute(attended, SECT, ring(NS, 1))
    near, _ = lax.optimization_barrier((near, attended))
    leave = [(s, (s + 1) % NX + s // NX * NX) for s in range(NS) if s % NX >= wrap - 1]
    leaving = jnp.where(my_x == wrap, near, rest)
    far = lax.ppermute(leaving, SECT, leave)
    by_near = ((my_x > 0) & (my_x < wrap)).astype(jnp.int32)
    place = jnp.stack([my_index, my_z, by_near])
    query_new, keyval_new, max_new, sum_new, out_new = layer(
        place, spans, attended_sent, direct, near, far, norm_gain, weights
    )
    return (query_new[None], keyval_new[None], max_new.T[None], sum_new.T[None], out_new[None])


def solution(mesh):
    fine = Mesh(mesh.devices.reshape(2, NX, NY, NZ, NC), (*SECT, *CTX))
    rows = P(SECT, CTX, None)
    return jax.shard_map(
        per_device,
        mesh=fine,
        in_specs=(*[rows] * 6, P(), P(SECT, None), rows, rows, P(SECT, None, CTX)),
        out_specs=(rows,) * 5,
        check_vma=False,
    )
```

time: 460 us -> 200 us (0.43)
  waiting for transfers between devices: 405 us -> 109 us
  starting transfers between devices: 16.7 us -> 49.3 us
  Pallas kernels: 0 us -> 18.5 us
  matrix products: 11.4 us -> 0 us
    all_gather x3 -> x1, waiting for transfers between devices: 299 us -> 0.01 us  [per_device(): weights = lax.all_gather(shards, ('y', 'c'), axis=0, tiled=True)]
    ppermute x3 -> x10, starting transfers between devices: 16.6 us -> 41.4 us  [the longest x4 19 us: per_device(): out_parts.append(lax.ppermute(w_out[0].T, (*SECT, 'zl'), pairs))]
    pallas_call x0 -> x2, Pallas kernels: none -> 18.5 us  [the longest x1 13.8 us: layer(): pl.pallas_call(layer_kernel, out_shape=out_shape, grid_spec=pltpu.Prefetc...]
    dot_general x9 -> x0, matrix products: 11.4 us -> none  [the longest x2 5.86 us: add_rows(): return jnp.dot(normed, shard_rows, preferred_element_type=jnp.float32)]
    all_to_all x0 -> x1, starting transfers between devices: none -> 7.93 us  [per_device(): lax.all_to_all(next_copies, 'zl', 0, 0, tiled=True)]
    ppermute x3 -> x10, waiting for transfers between devices: 104 us -> 109 us  [the longest x1 79.4 us: per_device(): attended_sent = lax.ppermute(attended, SECT, ring(NS, 1))]
  transfers between devices with their start and end apart: 6 -> 12, of which waited for: 5 -> 5; matrix products, arithmetic and copies ran while one was open for 4% -> 2% of each run, Pallas kernels for 0% -> 2%
where the time goes in v1:
time: 200 us; the launch traced here: 199 us
  waiting for transfers between devices  109 us (54%)
  starting transfers between devices  49.3 us (25%)
  Pallas kernels  18.5 us (9%)
  between operations  14.2 us (7%)
  local copies, waits for them, and re-layouts  4.51 us (2%)
  other arithmetic  3.43 us (2%)
    ppermute x1, waiting for transfers between devices, per_device(): attended_sent = lax.ppermute(attended, SECT, ring(NS, 1))  79.4 us
    ppermute x4, starting transfers between devices, per_device(): out_parts.append(lax.ppermute(w_out[0].T, (*SECT, 'zl'), pairs))  19 us
    ppermute x1, waiting for transfers between devices, per_device(): far = lax.ppermute(leaving, SECT, leave)  16.9 us
    pallas_call x1, Pallas kernels, layer(): pl.pallas_call(layer_kernel, out_shape=out_shape, grid_spec=pltpu.Prefetc...  13.8 us
    ppermute x1, waiting for transfers between devices, per_device(): near = lax.ppermute(rest, SECT, turn)  8.89 us
    all_to_all x1, starting transfers between devices, per_device(): lax.all_to_all(next_copies, 'zl', 0, 0, tiled=True)  7.93 us
    ppermute x1, starting transfers between devices, per_device(): near_block = lax.ppermute(keyvals[0], CTX, ring(count, -1))  7.26 us
    ppermute x1, starting transfers between devices, per_device(): far_block = lax.ppermute(keyvals[0], CTX, ring(count, -2))  7.1 us
  transfers between devices with their start and end apart: 12, of which 5 were waited for; matrix products, arithmetic and copies ran while one was open for 2% of the time, Pallas kernels for 2%

profile of v1, /device:TPU:1, one launch (start us, length us, event | category | flops | bytes accessed | tf_op | source)
XLA Modules:
  0.0 199.2 jit_solution(1240629348889198550)
XLA Ops:
  7.2 0.0 copy-start.8
  7.2 0.9 pad_maximum_fusion
  8.1 0.8 broadcast_in_dim.18
  8.8 0.0 copy-start.7
  8.8 0.0 copy-start
  8.9 7.9 %all-to-all-start = ((bf16[4,64,768]{2,1,0:T(8,128)(2,1)}), bf16[4,64,768]{2,1,0:T(8,128)(2,1)S(1)}, u32[]{:S(2)}, u32[]{:S(2)}) async-start(bf16[4,64,768]{2,1,0:T(8,128)(2,1)} %broadcast_in_dim.18), calls=%async_computation | async-start | bytes 786432 | tf_op jit(solution)/shard_map/all_to_all | solution.py:269
  16.8 0.0 all-gather.2.cloned.1.call-start
  16.8 0.0 copy-done.8
  16.8 6.1 %collective-permute-start.9 = (bf16[64,512]{1,0:T(8,128)(2,1)S(1)}, bf16[64,512]{1,0:T(8,128)(2,1)S(1)}, u32[]{:S(2)}, u32[]{:S(2)}) collective-permute-start(bf16[64,512]{1,0:T(8,128)(2,1)S(1)} %bitcast.48), channel_id=1, source_target_pairs={{0,70},{2,64},{4,66},{6,68},{64,134},{66,128},{68,130},{70,132},{1... | collective-permute-start | bytes 196616 | tf_op jit(solution)/shard_map/ppermute | solution.py:263
  22.9 2.2 %collective-permute-start.8 = (bf16[64,512]{1,0:T(8,128)(2,1)S(1)}, bf16[64,512]{1,0:T(8,128)(2,1)S(1)}, u32[]{:S(2)}, u32[]{:S(2)}) collective-permute-start(bf16[64,512]{1,0:T(8,128)(2,1)S(1)} %bitcast.49), channel_id=1, source_target_pairs={{0,68},{2,70},{4,64},{6,66},{64,132},{66,134},{68,128},{70,130},{1... | collective-permute-start | bytes 196616 | tf_op jit(solution)/shard_map/ppermute | solution.py:263
  25.1 3.7 %collective-permute-start.7 = (bf16[64,512]{1,0:T(8,128)(2,1)S(1)}, bf16[64,512]{1,0:T(8,128)(2,1)S(1)}, u32[]{:S(2)}, u32[]{:S(2)}) collective-permute-start(bf16[64,512]{1,0:T(8,128)(2,1)S(1)} %bitcast.50), channel_id=1, source_target_pairs={{0,66},{2,68},{4,70},{6,64},{64,130},{66,132},{68,134},{70,128},{1... | collective-permute-start | bytes 196616 | tf_op jit(solution)/shard_map/ppermute | solution.py:263
  28.8 7.0 %collective-permute-start.6 = (bf16[64,512]{1,0:T(8,128)(2,1)S(1)}, bf16[64,512]{1,0:T(8,128)(2,1)S(1)}, u32[]{:S(2)}, u32[]{:S(2)}) collective-permute-start(bf16[64,512]{1,0:T(8,128)(2,1)S(1)} %bitcast.51), channel_id=1, source_target_pairs={{0,64},{2,66},{4,68},{6,70},{64,128},{66,130},{68,132},{70,134},{1... | collective-permute-start | bytes 196616 | tf_op jit(solution)/shard_map/ppermute | solution.py:263
  35.8 0.6 collective-permute-done.9
  36.4 0.0 collective-permute-done.8
  36.4 0.0 collective-permute-done.7
  36.4 3.4 %collective-permute-done.6 = bf16[64,512]{1,0:T(8,128)(2,1)S(1)} collective-permute-done((bf16[64,512]{1,0:T(8,128)(2,1)S(1)}, bf16[64,512]{1,0:T(8,128)(2,1)S(1)}, u32[]{:S(2)}, u32[]{:S(2)}) %collective-permute-start.6) | collective-permute-done | bytes 65568 | tf_op jit(solution)/shard_map/ppermute | solution.py:263
  39.9 0.0 all-to-all-done
  39.9 0.9 maximum_maximum_fusion
  40.8 0.0 all-gather.2.cloned.1.call-update
  40.8 0.0 copy-done.7
  40.8 7.1 %collective-permute-start = (bf16[256,256]{1,0:T(8,128)(2,1)S(1)}, bf16[256,256]{1,0:T(8,128)(2,1)S(1)}, u32[]{:S(2)}, u32[]{:S(2)}) collective-permute-start(bf16[256,256]{1,0:T(8,128)(2,1)S(1)} %bitcast.45), channel_id=1, source_target_pairs={{0,62},{1,63},{2,0},{3,1},{4,2},{5,3},{6,4},{7,5},{8,6},{9,7},{10,... | collective-permute-start | bytes 393224 | tf_op jit(solution)/shard_map/ppermute | solution.py:265
  47.9 7.3 %collective-permute-start.1 = (bf16[256,256]{1,0:T(8,128)(2,1)S(1)}, bf16[256,256]{1,0:T(8,128)(2,1)S(1)}, u32[]{:S(2)}, u32[]{:S(2)}) collective-permute-start(bf16[256,256]{1,0:T(8,128)(2,1)S(1)} %bitcast.46), channel_id=1, source_target_pairs={{0,63},{1,0},{2,1},{3,2},{4,3},{5,4},{6,5},{7,6},{8,7},{9,8},{10,9... | collective-permute-start | bytes 393224 | tf_op jit(solution)/shard_map/ppermute | solution.py:264
  55.2 0.0 copy-done
  55.2 0.9 slice_bitcast_fusion.1
  56.1 1.3 collective-permute-start.4
  57.5 1.2 slice_bitcast_fusion
  58.7 1.9 collective-permute-start.3
  60.6 0.0 collective-permute-done.far_ref
  60.6 0.0 copy-start.5
  60.6 0.0 collective-permute-done.1.near_ref
  60.7 0.0 copy-start.6
  60.7 0.6 copy-done.5
  61.3 0.0 copy-done.6
  61.3 4.7 %attend.1 = bf16[256,512]{1,0:T(8,128)(2,1)} custom-call(s32[1]{0:T(128)} %bitcast.index_ref, s32[2,64]{1,0:T(2,128)} %bitcast.39, bf16[256,512]{1,0:T(8,128)(2,1)} %bitcast.36, bf16[256,256]{1,0:T(8,128)(2,1)} %copy-done.5, bf16[256,256]{1,0:T(8,128)(2,1)} %copy-done.6, f32[4,256]{1,0:T(4,128)} %bitcast.41, f32[4,256]{1,0:T(4,128)} %bitcast.42, ...), custom_call_target="tpu_custom_call" | custom-call | tf_op jit(solution)/shard_map/attend/pallas_call | solution.py:70
  66.0 0.0 copy-start.4
  66.0 8.9 %collective-permute-done.4.near_ref = bf16[96,4096]{1,0:T(8,128)(2,1)S(1)} collective-permute-done((bf16[96,4096]{1,0:T(8,128)(2,1)}, bf16[96,4096]{1,0:T(8,128)(2,1)S(1)}, u32[]{:S(2)}, u32[]{:S(2)}) %collective-permute-start.4) | collective-permute-done | bytes 786464 | tf_op jit(solution)/shard_map/ppermute | solution.py:277
  74.9 1.1 broadcast_select_fusion
  75.9 1.3 collective-permute-start.5
  77.2 0.0 copy-done.4
  77.2 3.5 %collective-permute-start.2 = (bf16[256,512]{1,0:T(8,128)(2,1)S(1)}, bf16[256,512]{1,0:T(8,128)(2,1)S(1)}, u32[]{:S(2)}, u32[]{:S(2)}) collective-permute-start(bf16[256,512]{1,0:T(8,128)(2,1)S(1)} %copy-done.4), channel_id=1, source_target_pairs={{0,64},{64,128},{128,192},{192,256},{256,320},{320,384},{384,448},... | collective-permute-start | bytes 786440 | tf_op jit(solution)/shard_map/ppermute | solution.py:283
  80.8 0.6 pad_add_fusion.place_ref
  81.4 79.4 %collective-permute-done.2.att_ref = bf16[256,512]{1,0:T(8,128)(2,1)S(1)} collective-permute-done((bf16[256,512]{1,0:T(8,128)(2,1)S(1)}, bf16[256,512]{1,0:T(8,128)(2,1)S(1)}, u32[]{:S(2)}, u32[]{:S(2)}) %collective-permute-start.2) | collective-permute-done | bytes 262176 | tf_op jit(solution)/shard_map/ppermute | solution.py:283
  160.7 0.0 collective-permute-done.3.direct_ref
  160.7 16.9 %collective-permute-done.5.far_ref = bf16[96,4096]{1,0:T(8,128)(2,1)S(1)} collective-permute-done((bf16[96,4096]{1,0:T(8,128)(2,1)}, bf16[96,4096]{1,0:T(8,128)(2,1)S(1)}, u32[]{:S(2)}, u32[]{:S(2)}) %collective-permute-start.5) | collective-permute-done | bytes 786464 | tf_op jit(solution)/shard_map/ppermute | solution.py:287
  177.7 0.0 copy-done.1
  177.7 0.0 copy-done.3
  177.7 0.9 copy-done.2
  178.6 13.8 %layer.1 = (bf16[256,512]{1,0:T(8,128)(2,1)}, bf16[256,256]{1,0:T(8,128)(2,1)}, f32[4,256]{1,0:T(4,128)}, f32[4,256]{1,0:T(4,128)}, f32[256,512]{1,0:T(8,128)}) custom-call(s32[3]{0:T(128)} %pad_add_fusion.place_ref, s32[2,64]{1,0:T(2,128)} %bitcast.40, bf16[256,512]{1,0:T(8,128)(2,1)} %copy-done.3, bf16[160,4096]{1,0:T(8,128)(2,1)} %collective-permute-done.3.direct_ref, ...), custom_call_target="tpu_custom_call" | custom-call | tf_op jit(solution)/shard_map/layer/pallas_call | solution.py:211
  (4 shorter events, 0.0 us)
Async XLA Ops:
  7.2 9.6 %copy-start.8 = (bf16[1,512,64]{1,2,0:T(8,128)(2,1)S(1)}, bf16[1,512,64]{1,2,0:T(8,128)(2,1)}, u32[]{:S(2)}) copy-start(bf16[1,512,64]{1,2,0:T(8,128)(2,1)} %param.21) | copy-start | bytes 196612
  8.8 32.0 %copy-start.7 = (bf16[1,256,256]{2,1,0:T(8,128)(2,1)S(1)}, bf16[1,256,256]{2,1,0:T(8,128)(2,1)}, u32[]{:S(2)}) copy-start(bf16[1,256,256]{2,1,0:T(8,128)(2,1)} %param.13) | copy-start | bytes 393220
  8.8 46.3 %copy-start = (bf16[1,256,4096]{2,1,0:T(8,128)(2,1)S(1)}, bf16[1,256,4096]{2,1,0:T(8,128)(2,1)}, u32[]{:S(2)}) copy-start(bf16[1,256,4096]{2,1,0:T(8,128)(2,1)} %param.11) | copy-start | bytes 6291460
  8.9 31.0 %all-to-all-start = ((bf16[4,64,768]{2,1,0:T(8,128)(2,1)}), bf16[4,64,768]{2,1,0:T(8,128)(2,1)S(1)}, u32[]{:S(2)}, u32[]{:S(2)}) async-start(bf16[4,64,768]{2,1,0:T(8,128)(2,1)} %broadcast_in_dim.18), calls=%async_computation | async-start | bytes 786432 | tf_op jit(solution)/shard_map/all_to_all | solution.py:269
  16.8 160.9 %all-gather.2.cloned.1.call-start = ((), (), s32[]{:S(2)}) async-start(), calls=%async_computation.1 | async-start | bytes 11141120 | tf_op jit(solution)/shard_map/all_gather | solution.py:271
  16.8 19.6 %collective-permute-start.9 = (bf16[64,512]{1,0:T(8,128)(2,1)S(1)}, bf16[64,512]{1,0:T(8,128)(2,1)S(1)}, u32[]{:S(2)}, u32[]{:S(2)}) collective-permute-start(bf16[64,512]{1,0:T(8,128)(2,1)S(1)} %bitcast.48), channel_id=1, source_target_pairs={{0,70},{2,64},{4,66},{6,68},{64,134},{66,128},{68,130},{70,132},{1... | collective-permute-start | bytes 196616 | tf_op jit(solution)/shard_map/ppermute | solution.py:263
  22.9 13.5 %collective-permute-start.8 = (bf16[64,512]{1,0:T(8,128)(2,1)S(1)}, bf16[64,512]{1,0:T(8,128)(2,1)S(1)}, u32[]{:S(2)}, u32[]{:S(2)}) collective-permute-start(bf16[64,512]{1,0:T(8,128)(2,1)S(1)} %bitcast.49), channel_id=1, source_target_pairs={{0,68},{2,70},{4,64},{6,66},{64,132},{66,134},{68,128},{70,130},{1... | collective-permute-start | bytes 196616 | tf_op jit(solution)/shard_map/ppermute | solution.py:263
  25.1 11.3 %collective-permute-start.7 = (bf16[64,512]{1,0:T(8,128)(2,1)S(1)}, bf16[64,512]{1,0:T(8,128)(2,1)S(1)}, u32[]{:S(2)}, u32[]{:S(2)}) collective-permute-start(bf16[64,512]{1,0:T(8,128)(2,1)S(1)} %bitcast.50), channel_id=1, source_target_pairs={{0,66},{2,68},{4,70},{6,64},{64,130},{66,132},{68,134},{70,128},{1... | collective-permute-start | bytes 196616 | tf_op jit(solution)/shard_map/ppermute | solution.py:263
  28.8 11.0 %collective-permute-start.6 = (bf16[64,512]{1,0:T(8,128)(2,1)S(1)}, bf16[64,512]{1,0:T(8,128)(2,1)S(1)}, u32[]{:S(2)}, u32[]{:S(2)}) collective-permute-start(bf16[64,512]{1,0:T(8,128)(2,1)S(1)} %bitcast.51), channel_id=1, source_target_pairs={{0,64},{2,66},{4,68},{6,70},{64,128},{66,130},{68,132},{70,134},{1... | collective-permute-start | bytes 196616 | tf_op jit(solution)/shard_map/ppermute | solution.py:263
  40.8 19.8 %collective-permute-start = (bf16[256,256]{1,0:T(8,128)(2,1)S(1)}, bf16[256,256]{1,0:T(8,128)(2,1)S(1)}, u32[]{:S(2)}, u32[]{:S(2)}) collective-permute-start(bf16[256,256]{1,0:T(8,128)(2,1)S(1)} %bitcast.45), channel_id=1, source_target_pairs={{0,62},{1,63},{2,0},{3,1},{4,2},{5,3},{6,4},{7,5},{8,6},{9,7},{10,... | collective-permute-start | bytes 393224 | tf_op jit(solution)/shard_map/ppermute | solution.py:265
  47.9 12.7 %collective-permute-start.1 = (bf16[256,256]{1,0:T(8,128)(2,1)S(1)}, bf16[256,256]{1,0:T(8,128)(2,1)S(1)}, u32[]{:S(2)}, u32[]{:S(2)}) collective-permute-start(bf16[256,256]{1,0:T(8,128)(2,1)S(1)} %bitcast.46), channel_id=1, source_target_pairs={{0,63},{1,0},{2,1},{3,2},{4,3},{5,4},{6,5},{7,6},{8,7},{9,8},{10,9... | collective-permute-start | bytes 393224 | tf_op jit(solution)/shard_map/ppermute | solution.py:264
  56.1 18.7 %collective-permute-start.4 = (bf16[96,4096]{1,0:T(8,128)(2,1)}, bf16[96,4096]{1,0:T(8,128)(2,1)S(1)}, u32[]{:S(2)}, u32[]{:S(2)}) collective-permute-start(bf16[96,4096]{1,0:T(8,128)(2,1)} %slice_bitcast_fusion.1), channel_id=1, source_target_pairs={{0,64},{64,128},{256,320},{320,384},{192,448},{448,192},{1,65},{65... | collective-permute-start | bytes 2359304 | tf_op jit(solution)/shard_map/ppermute | solution.py:277
  58.7 102.0 %collective-permute-start.3 = (bf16[160,4096]{1,0:T(8,128)(2,1)}, bf16[160,4096]{1,0:T(8,128)(2,1)}, u32[]{:S(2)}, u32[]{:S(2)}) collective-permute-start(bf16[160,4096]{1,0:T(8,128)(2,1)} %slice_bitcast_fusion), channel_id=1, source_target_pairs={{0,64},{64,128},{128,192},{192,256},{256,320},{320,384},{384,448},... | collective-permute-start | bytes 3932168 | tf_op jit(solution)/shard_map/ppermute | solution.py:278
  60.6 0.7 copy-start.5
  60.7 0.7 copy-start.6
  66.0 11.2 %copy-start.4 = (bf16[256,512]{1,0:T(8,128)(2,1)S(1)}, bf16[256,512]{1,0:T(8,128)(2,1)}, u32[]{:S(2)}) copy-start(bf16[256,512]{1,0:T(8,128)(2,1)} %attend.1) | copy-start | bytes 786436
  74.9 102.8 %copy-start.1 = (bf16[96,4096]{1,0:T(8,128)(2,1)}, bf16[96,4096]{1,0:T(8,128)(2,1)S(1)}, u32[]{:S(2)}) copy-start(bf16[96,4096]{1,0:T(8,128)(2,1)S(1)} %collective-permute-done.4.near_ref) | copy-start | bytes 2359300
  75.9 101.7 %collective-permute-start.5 = (bf16[96,4096]{1,0:T(8,128)(2,1)}, bf16[96,4096]{1,0:T(8,128)(2,1)S(1)}, u32[]{:S(2)}, u32[]{:S(2)}) collective-permute-start(bf16[96,4096]{1,0:T(8,128)(2,1)} %broadcast_select_fusion), channel_id=1, source_target_pairs={{128,192},{192,0},{384,448},{448,256},{129,193},{193,1},{385,449},... | collective-permute-start | bytes 2359304 | tf_op jit(solution)/shard_map/ppermute | solution.py:287
  77.2 83.5 %collective-permute-start.2 = (bf16[256,512]{1,0:T(8,128)(2,1)S(1)}, bf16[256,512]{1,0:T(8,128)(2,1)S(1)}, u32[]{:S(2)}, u32[]{:S(2)}) collective-permute-start(bf16[256,512]{1,0:T(8,128)(2,1)S(1)} %copy-done.4), channel_id=1, source_target_pairs={{0,64},{64,128},{128,192},{192,256},{256,320},{320,384},{384,448},... | collective-permute-start | bytes 786440 | tf_op jit(solution)/shard_map/ppermute | solution.py:283
  160.7 17.0 %copy-start.3 = (bf16[256,512]{1,0:T(8,128)(2,1)}, bf16[256,512]{1,0:T(8,128)(2,1)S(1)}, u32[]{:S(2)}) copy-start(bf16[256,512]{1,0:T(8,128)(2,1)S(1)} %collective-permute-done.2.att_ref) | copy-start | bytes 786436
  177.7 0.9 copy-start.2
Sparse Core Ops, SparseCore 0:
  40.9 72.1 all-gather.1

commit v2 on v1

--- a/solution.py
+++ b/solution.py
@@ -15,7 +15,7 @@
 SHARD = 64
 PAIR = 2
 NX = 4
-CUT = 160
+CUT = 144
 BLOCK = NZ * NC * SHARD
 NQ = QHEADS * HEAD
 NKV = 2 * HEAD
@@ -77,15 +77,14 @@
     )(my_index, spans, *operands)
 
 
-def in_order(w_ref, base, slots):
+def in_order(w_ref):
     parts = []
-    for z in range(NZ):
-        for c in range(NC):
-            start = base + (c * NZ + slots[z]) * SHARD
-            if not isinstance(start, int):
-                start = pl.multiple_of(start, SHARD)
-            parts.append(w_ref[pl.ds(start, SHARD), :])
-    return parts
+    for y in range(w_ref.shape[0] // BLOCK):
+        for z in range(NZ):
+            for c in range(NC):
+                start = ((y * NC + c) * NZ + z) * SHARD
+                parts.append(w_ref[start : start + SHARD, :])
+    return jnp.concatenate(parts, axis=0)
 
 
 def layer_kernel(
@@ -114,21 +113,16 @@
 
     @pl.when(step < half)
     def _():
-        slots = [lax.rem(place_ref[1] - z + NZ, NZ) for z in range(NZ)]
-
         def part(w_ref, cols):
-            pieces = []
-            for k in range(PAIR):
-                pieces += in_order(w_ref, k * BLOCK, slots)
             return lax.dot_general(
                 att_ref[:, cols],
-                jnp.concatenate(pieces, axis=0),
+                in_order(w_ref),
                 (((1,), (1,)), ((), ())),
                 preferred_element_type=jnp.float32,
             )
 
         projected = part(out_a_ref, slice(0, NQ // 2)) + part(out_b_ref, slice(NQ // 2, NQ))
-        by_near = place_ref[2] > 0
+        by_near = place_ref[1] > 0
         routed = jnp.where(by_near, near_ref[...], far_ref[...])
         resid = jnp.concatenate([direct_ref[...], routed], axis=0)
         finished = (resid.astype(jnp.float32) + projected).astype(jnp.bfloat16)
@@ -156,13 +150,8 @@
 
     @pl.when(step >= half)
     def _():
-        pieces = []
-        for k in range(PAIR):
-            pieces += in_order(next_ref, k * BLOCK, range(NZ))
         total = jnp.dot(
-            rows_ref[step - half],
-            jnp.concatenate(pieces, axis=0),
-            preferred_element_type=jnp.float32,
+            rows_ref[step - half], in_order(next_ref), preferred_element_type=jnp.float32
         )
 
         @pl.when(step == half)
@@ -251,42 +240,34 @@
 ):
     count = NY * NZ * NC
     my_index = lax.axis_index(CTX).astype(jnp.int32)
-    my_z = lax.axis_index("zl").astype(jnp.int32)
     my_x = lax.axis_index("x").astype(jnp.int32)
     spans = span_pair.T
 
-    out_parts = []
-    for k in range(NZ):
-        pairs = [
-            (s * NZ + z, (s + 1) % NS * NZ + (z + k) % NZ) for s in range(NS) for z in range(NZ)
-        ]
-        out_parts.append(lax.ppermute(w_out[0].T, (*SECT, "zl"), pairs))
+    out_shard = lax.ppermute(w_out[0].T, SECT, ring(NS, 1))
+    next_shard = jnp.concatenate([w_query[0], w_keyval[0]], axis=1)
+
+    def along_z(shard):
+        copies = jnp.broadcast_to(shard, (NZ, *shard.shape))
+        return lax.all_to_all(copies, "zl", 0, 0, tiled=True).reshape(NZ * SHARD, -1)
+
+    next_rows = along_z(next_shard)
+    out_rows = along_z(out_shard)
+    shards = jnp.concatenate([next_rows, out_rows], axis=1)
+    weights = lax.all_gather(shards, ("y", "c"), axis=0, tiled=True)
+
+    turn = [(s, (s + 1) % NX + s // NX * NX) for s in range(NS)]
+    near = lax.ppermute(resid[0, CUT:], SECT, turn)
+    direct = lax.ppermute(resid[0, :CUT], SECT, ring(NS, 1))
     near_block = lax.ppermute(keyvals[0], CTX, ring(count, -1))
     far_block = lax.ppermute(keyvals[0], CTX, ring(count, -2))
-
-    next_shard = jnp.concatenate([w_query[0], w_keyval[0]], axis=1)
-    next_copies = jnp.broadcast_to(next_shard, (NZ, SHARD, NQ + NKV))
-    next_rows = lax.all_to_all(next_copies, "zl", 0, 0, tiled=True).reshape(NZ * SHARD, NQ + NKV)
-    shards = jnp.concatenate([next_rows, jnp.concatenate(out_parts)], axis=1)
-    weights = lax.all_gather(shards, ("y", "c"), axis=0, tiled=True)
-
-    rest = resid[0, CUT:]
-    wrap = NX - 1
-    turn = [(s, s + 1) for s in range(NS) if s % NX < wrap - 1]
-    turn += [(s, (s + NX) % NS) for s in range(NS) if s % NX == wrap]
-    near = lax.ppermute(rest, SECT, turn)
-    direct = lax.ppermute(resid[0, :CUT], SECT, ring(NS, 1))
     attended = attend(
         my_index.reshape(1), spans, queries[0], far_block, near_block,
         run_max[0].T, run_sum[0].T, run_out[0],
     )
     attended_sent = lax.ppermute(attended, SECT, ring(NS, 1))
-    near, _ = lax.optimization_barrier((near, attended))
-    leave = [(s, (s + 1) % NX + s // NX * NX) for s in range(NS) if s % NX >= wrap - 1]
-    leaving = jnp.where(my_x == wrap, near, rest)
-    far = lax.ppermute(leaving, SECT, leave)
-    by_near = ((my_x > 0) & (my_x < wrap)).astype(jnp.int32)
-    place = jnp.stack([my_index, my_z, by_near])
+    leaving, _ = lax.optimization_barrier((near, attended))
+    far = lax.ppermute(leaving, SECT, [(0, NX), (NX, 0)])
+    place = jnp.stack([my_index, (my_x > 0).astype(jnp.int32)])
     query_new, keyval_new, max_new, sum_new, out_new = layer(
         place, spans, attended_sent, direct, near, far, norm_gain, weights
     )

time: 200 us -> 159 us (0.80)
  waiting for transfers between devices: 109 us -> 58.9 us
  blocking collectives: 0 us -> 11.4 us
  starting transfers between devices: 49.3 us -> 47 us
    ppermute x1, waiting for transfers between devices: 79.4 us -> 39.1 us  [per_device(): attended_sent = lax.ppermute(attended, SECT, ring(NS, 1))]
    ppermute x6 -> x3, waiting for transfers between devices: 29.9 us -> 11.6 us  [the longest x1 11.6 us: per_device(): out_shard = lax.ppermute(w_out[0].T, SECT, ring(NS, 1))]
    all_to_all x0 -> x1, blocking collectives: none -> 11.4 us  [along_z(): lax.all_to_all(copies, 'zl', 0, 0, tiled=True).reshape(NZ * SHARD, -1)]
    ppermute x1, starting transfers between devices: 7.1 us -> 12 us  [per_device(): far_block = lax.ppermute(keyvals[0], CTX, ring(count, -2))]
    all_to_all x1, waiting for transfers between devices: 0.01 us -> 4.79 us  [along_z(): lax.all_to_all(copies, 'zl', 0, 0, tiled=True).reshape(NZ * SHARD, -1)]
    ppermute x1, starting transfers between devices: 7.26 us -> 3.31 us  [per_device(): near_block = lax.ppermute(keyvals[0], CTX, ring(count, -1))]
    ppermute x1, waiting for transfers between devices: 0.01 us -> 3.33 us  [per_device(): near_block = lax.ppermute(keyvals[0], CTX, ring(count, -1))]
    all_to_all x1, starting transfers between devices: 7.93 us -> 4.8 us  [along_z(): lax.all_to_all(copies, 'zl', 0, 0, tiled=True).reshape(NZ * SHARD, -1)]
  transfers between devices with their start and end apart: 12 -> 9, of which waited for: 5 -> 4; matrix products, arithmetic and copies ran while one was open for 2% -> 2% of each run, Pallas kernels for 2% -> 3%
where the time goes in v2:
time: 159 us; the launch traced here: 156 us
  waiting for transfers between devices  58.9 us (37%)
  starting transfers between devices  47 us (30%)
  Pallas kernels  18.5 us (12%)
  between operations  14.2 us (9%)
  blocking collectives  11.4 us (7%)
  local copies, waits for them, and re-layouts  3.92 us (2%)
  other arithmetic  2.43 us (2%)
    ppermute x1, waiting for transfers between devices, per_device(): attended_sent = lax.ppermute(attended, SECT, ring(NS, 1))  39.1 us
    ppermute x1, starting transfers between devices, per_device(): far = lax.ppermute(leaving, SECT, [(0, NX), (NX, 0)])  17.1 us
    pallas_call x1, Pallas kernels, layer(): pl.pallas_call(layer_kernel, out_shape=out_shape, grid_spec=pltpu.Prefetc...  13.8 us
    ppermute x1, starting transfers between devices, per_device(): far_block = lax.ppermute(keyvals[0], CTX, ring(count, -2))  12 us
    ppermute x1, waiting for transfers between devices, per_device(): out_shard = lax.ppermute(w_out[0].T, SECT, ring(NS, 1))  11.6 us
    all_to_all x1, blocking collectives, along_z(): lax.all_to_all(copies, 'zl', 0, 0, tiled=True).reshape(NZ * SHARD, -1)  11.4 us
    all_to_all x1, starting transfers between devices, along_z(): lax.all_to_all(copies, 'zl', 0, 0, tiled=True).reshape(NZ * SHARD, -1)  4.8 us
    all_to_all x1, waiting for transfers between devices, along_z(): lax.all_to_all(copies, 'zl', 0, 0, tiled=True).reshape(NZ * SHARD, -1)  4.79 us
  transfers between devices with their start and end apart: 9, of which 4 were waited for; matrix products, arithmetic and copies ran while one was open for 2% of the time, Pallas kernels for 3%

profile of v2, /device:TPU:1, one launch (start us, length us, event | category | flops | bytes accessed | tf_op | source)
XLA Modules:
  0.0 156.3 jit_solution(2443127712320886018)
XLA Ops:
  7.2 3.9 %collective-permute-start.6 = (bf16[64,512]{1,0:T(8,128)(2,1)}, bf16[64,512]{1,0:T(8,128)(2,1)S(1)}, u32[]{:S(2)}, u32[]{:S(2)}) collective-permute-start(bf16[64,512]{1,0:T(8,128)(2,1)} %bitcast.47), channel_id=1, source_target_pairs={{0,64},{64,128},{128,192},{192,256},{256,320},{320,384},{384,448},... | collective-permute-start | bytes 196616 | tf_op jit(solution)/shard_map/ppermute | solution.py:246
  11.1 11.6 %collective-permute-done.6 = bf16[64,512]{1,0:T(8,128)(2,1)S(1)} collective-permute-done((bf16[64,512]{1,0:T(8,128)(2,1)}, bf16[64,512]{1,0:T(8,128)(2,1)S(1)}, u32[]{:S(2)}, u32[]{:S(2)}) %collective-permute-start.6) | collective-permute-done | bytes 65568 | tf_op jit(solution)/shard_map/ppermute | solution.py:246
  22.7 0.7 broadcast_in_dim.22
  23.5 4.8 %all-to-all-start.1 = ((bf16[4,64,512]{2,1,0:T(8,128)(2,1)}), bf16[4,64,512]{2,1,0:T(8,128)(2,1)S(1)}, u32[]{:S(2)}, u32[]{:S(2)}) async-start(bf16[4,64,512]{2,1,0:T(8,128)(2,1)} %broadcast_in_dim.22), calls=%async_computation.1 | async-start | bytes 524288 | tf_op jit(solution)/shard_map/all_to_all | solution.py:251
  28.3 0.0 all-gather.2.cloned.1.call-start
  28.3 0.9 pad_maximum_fusion.1
  29.1 4.8 %all-to-all-done.1 = bf16[4,64,512]{2,1,0:T(8,128)(2,1)S(1)} async-done(((bf16[4,64,512]{2,1,0:T(8,128)(2,1)}), bf16[4,64,512]{2,1,0:T(8,128)(2,1)S(1)}, u32[]{:S(2)}, u32[]{:S(2)}) %all-to-all-start.1) | async-done | bytes 262176 | tf_op jit(solution)/shard_map/all_to_all | solution.py:251
  34.0 0.0 copy-start
  34.0 11.4 %all_to_all.10 = bf16[4,64,768]{2,1,0:T(8,128)(2,1)S(1)} all-to-all(bf16[4,64,768]{2,1,0:T(8,128)(2,1)S(1)} %broadcast_in_dim.21), channel_id=1, replica_groups=mesh['zh'=2,'x'=4,'y'=8,'zl'=4,'c'=2] {'zl'}, dimensions={0} | all-to-all | bytes 786432 | tf_op jit(solution)/shard_map/all_to_all | solution.py:251
  45.3 0.9 pad_maximum_fusion
  46.3 0.0 all-gather.2.cloned.1.call-update
  46.3 0.0 copy-done
  46.3 1.0 slice_bitcast_fusion.1
  47.3 0.0 copy-start.6
  47.3 2.0 %collective-permute-start.4 = (bf16[112,4096]{1,0:T(8,128)(2,1)}, bf16[112,4096]{1,0:T(8,128)(2,1)}, u32[]{:S(2)}, u32[]{:S(2)}) collective-permute-start(bf16[112,4096]{1,0:T(8,128)(2,1)} %slice_bitcast_fusion.1), channel_id=1, source_target_pairs={{0,64},{64,128},{128,192},{192,0},{256,320},{320,384},{384,448},{4... | collective-permute-start | bytes 2752520 | tf_op jit(solution)/shard_map/ppermute | solution.py:259
  49.3 0.1 slice_bitcast_fusion
  49.4 1.9 %collective-permute-start.3 = (bf16[144,4096]{1,0:T(8,128)(2,1)S(1)}, bf16[144,4096]{1,0:T(8,128)(2,1)S(1)}, u32[]{:S(2)}, u32[]{:S(2)}) collective-permute-start(bf16[144,4096]{1,0:T(8,128)(2,1)S(1)} %slice_bitcast_fusion), channel_id=1, source_target_pairs={{0,64},{64,128},{128,192},{192,256},{256,320},{320,384},{384,448},... | collective-permute-start | bytes 3538952 | tf_op jit(solution)/shard_map/ppermute | solution.py:260
  51.4 0.0 copy-done.6
  51.4 12.0 %collective-permute-start = (bf16[256,256]{1,0:T(8,128)(2,1)S(1)}, bf16[256,256]{1,0:T(8,128)(2,1)S(1)}, u32[]{:S(2)}, u32[]{:S(2)}) collective-permute-start(bf16[256,256]{1,0:T(8,128)(2,1)S(1)} %bitcast.44), channel_id=1, source_target_pairs={{0,62},{1,63},{2,0},{3,1},{4,2},{5,3},{6,4},{7,5},{8,6},{9,7},{10,... | collective-permute-start | bytes 393224 | tf_op jit(solution)/shard_map/ppermute | solution.py:262
  63.4 3.3 %collective-permute-start.1 = (bf16[256,256]{1,0:T(8,128)(2,1)S(1)}, bf16[256,256]{1,0:T(8,128)(2,1)S(1)}, u32[]{:S(2)}, u32[]{:S(2)}) collective-permute-start(bf16[256,256]{1,0:T(8,128)(2,1)S(1)} %bitcast.45), channel_id=1, source_target_pairs={{0,63},{1,0},{2,1},{3,2},{4,3},{5,4},{6,5},{7,6},{8,7},{9,8},{10,9... | collective-permute-start | bytes 393224 | tf_op jit(solution)/shard_map/ppermute | solution.py:261
  66.7 0.0 collective-permute-done.far_ref
  66.7 0.0 copy-start.4
  66.8 3.3 %collective-permute-done.1.near_ref = bf16[256,256]{1,0:T(8,128)(2,1)S(1)} collective-permute-done((bf16[256,256]{1,0:T(8,128)(2,1)S(1)}, bf16[256,256]{1,0:T(8,128)(2,1)S(1)}, u32[]{:S(2)}, u32[]{:S(2)}) %collective-permute-start.1) | collective-permute-done | bytes 131104 | tf_op jit(solution)/shard_map/ppermute | solution.py:261
  70.1 0.0 copy-start.5
  70.1 0.0 copy-done.4
  70.1 0.7 copy-done.5
  70.7 4.7 %attend.1 = bf16[256,512]{1,0:T(8,128)(2,1)} custom-call(s32[1]{0:T(128)} %bitcast.index_ref, s32[2,64]{1,0:T(2,128)} %bitcast.38, bf16[256,512]{1,0:T(8,128)(2,1)} %bitcast.35, bf16[256,256]{1,0:T(8,128)(2,1)} %copy-done.4, bf16[256,256]{1,0:T(8,128)(2,1)} %copy-done.5, f32[4,256]{1,0:T(4,128)} %bitcast.40, f32[4,256]{1,0:T(4,128)} %bitcast.41, ...), custom_call_target="tpu_custom_call" | custom-call | tf_op jit(solution)/shard_map/attend/pallas_call | solution.py:70
  75.4 0.0 collective-permute-done.4.near_ref
  75.4 17.1 %collective-permute-start.5 = (bf16[112,4096]{1,0:T(8,128)(2,1)}, bf16[112,4096]{1,0:T(8,128)(2,1)S(1)}, u32[]{:S(2)}, u32[]{:S(2)}) collective-permute-start(bf16[112,4096]{1,0:T(8,128)(2,1)} %collective-permute-done.4.near_ref), channel_id=1, source_target_pairs={{0,256},{256,0},{1,257},{257,1},{2,258},{258,2},{3,259},{259,3},{4... | collective-permute-start | bytes 2752520 | tf_op jit(solution)/shard_map/ppermute | solution.py:269
  92.5 1.9 %collective-permute-start.2 = (bf16[256,512]{1,0:T(8,128)(2,1)}, bf16[256,512]{1,0:T(8,128)(2,1)S(1)}, u32[]{:S(2)}, u32[]{:S(2)}) collective-permute-start(bf16[256,512]{1,0:T(8,128)(2,1)} %attend.1), channel_id=1, source_target_pairs={{0,64},{64,128},{128,192},{192,256},{256,320},{320,384},{384,448},... | collective-permute-start | bytes 786440 | tf_op jit(solution)/shard_map/ppermute | solution.py:267
  94.4 0.7 pad_add_fusion.place_ref
  95.1 39.1 %collective-permute-done.2.att_ref = bf16[256,512]{1,0:T(8,128)(2,1)S(1)} collective-permute-done((bf16[256,512]{1,0:T(8,128)(2,1)}, bf16[256,512]{1,0:T(8,128)(2,1)S(1)}, u32[]{:S(2)}, u32[]{:S(2)}) %collective-permute-start.2) | collective-permute-done | bytes 262176 | tf_op jit(solution)/shard_map/ppermute | solution.py:267
  134.2 0.0 copy-start.3
  134.2 0.0 collective-permute-done.3.direct_ref
  134.2 0.0 copy-start.1
  134.2 0.0 collective-permute-done.5.far_ref
  134.2 0.0 copy-start.2
  134.2 0.0 all-gather.2.cloned.1.call-done.out_a_ref.out_b_ref.next_ref
  134.3 0.6 copy-done.3
  134.9 0.4 copy-done.1
  135.3 0.3 copy-done.2
  135.7 13.8 %layer.1 = (bf16[256,512]{1,0:T(8,128)(2,1)}, bf16[256,256]{1,0:T(8,128)(2,1)}, f32[4,256]{1,0:T(4,128)}, f32[4,256]{1,0:T(4,128)}, f32[256,512]{1,0:T(8,128)}) custom-call(s32[2]{0:T(128)} %pad_add_fusion.place_ref, s32[2,64]{1,0:T(2,128)} %bitcast.39, bf16[256,512]{1,0:T(8,128)(2,1)} %copy-done.3, bf16[144,4096]{1,0:T(8,128)(2,1)} %copy-done.1, ...), custom_call_target="tpu_custom_call" | custom-call | tf_op jit(solution)/shard_map/layer/pallas_call | solution.py:200
  (1 shorter events, 0.0 us)
Async XLA Ops:
  7.2 15.6 %collective-permute-start.6 = (bf16[64,512]{1,0:T(8,128)(2,1)}, bf16[64,512]{1,0:T(8,128)(2,1)S(1)}, u32[]{:S(2)}, u32[]{:S(2)}) collective-permute-start(bf16[64,512]{1,0:T(8,128)(2,1)} %bitcast.47), channel_id=1, source_target_pairs={{0,64},{64,128},{128,192},{192,256},{256,320},{320,384},{384,448},... | collective-permute-start | bytes 196616 | tf_op jit(solution)/shard_map/ppermute | solution.py:246
  23.5 10.5 %all-to-all-start.1 = ((bf16[4,64,512]{2,1,0:T(8,128)(2,1)}), bf16[4,64,512]{2,1,0:T(8,128)(2,1)S(1)}, u32[]{:S(2)}, u32[]{:S(2)}) async-start(bf16[4,64,512]{2,1,0:T(8,128)(2,1)} %broadcast_in_dim.22), calls=%async_computation.1 | async-start | bytes 524288 | tf_op jit(solution)/shard_map/all_to_all | solution.py:251
  28.3 106.0 %all-gather.2.cloned.1.call-start = ((), (), s32[]{:S(2)}) async-start(), calls=%async_computation.2 | async-start | bytes 11141120 | tf_op jit(solution)/shard_map/all_gather | solution.py:256
  34.0 12.3 %copy-start = (bf16[1,256,4096]{2,1,0:T(8,128)(2,1)S(1)}, bf16[1,256,4096]{2,1,0:T(8,128)(2,1)}, u32[]{:S(2)}) copy-start(bf16[1,256,4096]{2,1,0:T(8,128)(2,1)} %param.11) | copy-start | bytes 6291460
  47.3 4.1 %copy-start.6 = (bf16[1,256,256]{2,1,0:T(8,128)(2,1)S(1)}, bf16[1,256,256]{2,1,0:T(8,128)(2,1)}, u32[]{:S(2)}) copy-start(bf16[1,256,256]{2,1,0:T(8,128)(2,1)} %param.13) | copy-start | bytes 393220
  47.3 28.1 %collective-permute-start.4 = (bf16[112,4096]{1,0:T(8,128)(2,1)}, bf16[112,4096]{1,0:T(8,128)(2,1)}, u32[]{:S(2)}, u32[]{:S(2)}) collective-permute-start(bf16[112,4096]{1,0:T(8,128)(2,1)} %slice_bitcast_fusion.1), channel_id=1, source_target_pairs={{0,64},{64,128},{128,192},{192,0},{256,320},{320,384},{384,448},{4... | collective-permute-start | bytes 2752520 | tf_op jit(solution)/shard_map/ppermute | solution.py:259
  49.4 84.8 %collective-permute-start.3 = (bf16[144,4096]{1,0:T(8,128)(2,1)S(1)}, bf16[144,4096]{1,0:T(8,128)(2,1)S(1)}, u32[]{:S(2)}, u32[]{:S(2)}) collective-permute-start(bf16[144,4096]{1,0:T(8,128)(2,1)S(1)} %slice_bitcast_fusion), channel_id=1, source_target_pairs={{0,64},{64,128},{128,192},{192,256},{256,320},{320,384},{384,448},... | collective-permute-start | bytes 3538952 | tf_op jit(solution)/shard_map/ppermute | solution.py:260
  51.4 15.4 %collective-permute-start = (bf16[256,256]{1,0:T(8,128)(2,1)S(1)}, bf16[256,256]{1,0:T(8,128)(2,1)S(1)}, u32[]{:S(2)}, u32[]{:S(2)}) collective-permute-start(bf16[256,256]{1,0:T(8,128)(2,1)S(1)} %bitcast.44), channel_id=1, source_target_pairs={{0,62},{1,63},{2,0},{3,1},{4,2},{5,3},{6,4},{7,5},{8,6},{9,7},{10,... | collective-permute-start | bytes 393224 | tf_op jit(solution)/shard_map/ppermute | solution.py:262
  63.4 6.7 %collective-permute-start.1 = (bf16[256,256]{1,0:T(8,128)(2,1)S(1)}, bf16[256,256]{1,0:T(8,128)(2,1)S(1)}, u32[]{:S(2)}, u32[]{:S(2)}) collective-permute-start(bf16[256,256]{1,0:T(8,128)(2,1)S(1)} %bitcast.45), channel_id=1, source_target_pairs={{0,63},{1,0},{2,1},{3,2},{4,3},{5,4},{6,5},{7,6},{8,7},{9,8},{10,9... | collective-permute-start | bytes 393224 | tf_op jit(solution)/shard_map/ppermute | solution.py:261
  66.7 3.4 %copy-start.4 = (bf16[256,256]{1,0:T(8,128)(2,1)}, bf16[256,256]{1,0:T(8,128)(2,1)S(1)}, u32[]{:S(2)}) copy-start(bf16[256,256]{1,0:T(8,128)(2,1)S(1)} %collective-permute-done.far_ref) | copy-start | bytes 393220
  70.1 0.7 copy-start.5
  75.4 58.8 %collective-permute-start.5 = (bf16[112,4096]{1,0:T(8,128)(2,1)}, bf16[112,4096]{1,0:T(8,128)(2,1)S(1)}, u32[]{:S(2)}, u32[]{:S(2)}) collective-permute-start(bf16[112,4096]{1,0:T(8,128)(2,1)} %collective-permute-done.4.near_ref), channel_id=1, source_target_pairs={{0,256},{256,0},{1,257},{257,1},{2,258},{258,2},{3,259},{259,3},{4... | collective-permute-start | bytes 2752520 | tf_op jit(solution)/shard_map/ppermute | solution.py:269
  92.5 41.7 %collective-permute-start.2 = (bf16[256,512]{1,0:T(8,128)(2,1)}, bf16[256,512]{1,0:T(8,128)(2,1)S(1)}, u32[]{:S(2)}, u32[]{:S(2)}) collective-permute-start(bf16[256,512]{1,0:T(8,128)(2,1)} %attend.1), channel_id=1, source_target_pairs={{0,64},{64,128},{128,192},{192,256},{256,320},{320,384},{384,448},... | collective-permute-start | bytes 786440 | tf_op jit(solution)/shard_map/ppermute | solution.py:267
  134.2 0.7 copy-start.3
  134.2 1.1 copy-start.1
  134.2 1.4 copy-start.2
Sparse Core Ops, SparseCore 0:
  46.4 72.9 all-gather.1
